TPU v7x, 256 devices: a whole 4x4x8 slice. The times are simulated.
256 devices in a mesh: rep: 8 (over x, z_lo), mp: 32 (over z_hi, y, core).
Axes of the slice: x: 4, y: 4, z: 8 (z_hi: 4, z_lo: 2; z = z_hi * 2 + z_lo), core: 2. Of those that a mesh axis runs over, the one named last changes fastest.
Arguments:
- tokens: bfloat16 [8, 2048, 5120], P('rep', 'mp'), may hold values from -6 to 6
- prompt_ids: int32 [8, 2048], P('rep', 'mp'), may hold values from 0 to 11, never falling along the last dimension, each value on 1 to 512 neighbouring positions
- modulation: float32 [8, 12, 3, 5120], P('rep'), may hold values from -4 to 4
- trainer_up: float32 [5120, 13824], P('mp', 'rep'), may hold values from -0.078125 to 0.078125
- trainer_down: float32 [13824, 5120], P('rep', 'mp'), may hold values from -0.0546875 to 0.0546875
Outputs:
- result: bfloat16 [8, 2048, 5120], P('rep', 'mp')
Inputs may be any that keep to these rules, and one draw needn't show every extreme that they name: `prompt_ids`: along each replica's 2048 tokens the prompt number never falls; each of the 12 prompts has at least one token, and one prompt has exactly a quarter of 2048.
All inputs are finite; a program needn't handle non-finite values.
Results may differ from a plain program's by a relative error of at most 0.023.
Values may be sent and summed in bfloat16 or wider, within the bound.
A program may use at most 192 MiB of HBM per device.

v0:
```python
import jax
import jax.numpy as jnp
import numpy as np
from jax import lax
from jax.sharding import Mesh, PartitionSpec as P

MP = ("mc", "core")


def local(tokens, prompt_ids, modulation, trainer_up, trainer_down):
    as_float = tokens[0].astype(jnp.float32)
    average = jnp.mean(as_float, axis=-1, keepdims=True)
    centred = as_float - average
    variance = jnp.mean(centred * centred, axis=-1, keepdims=True)
    normed = centred / jnp.sqrt(variance + 1e-06)
    prompts_here = modulation.shape[1]
    onehot = (prompt_ids[0][:, None] == jnp.arange(prompts_here, dtype=jnp.int32)[None, :]).astype(
        jnp.float32
    )
    chosen = jnp.einsum("tp,pkd->tkd", onehot, modulation[0], precision=lax.Precision.HIGHEST)
    shift = chosen[:, 0]
    scale = chosen[:, 1]
    gate = chosen[:, 2]
    xin = (normed * (1.0 + scale) + shift).astype(jnp.bfloat16)
    n_mp = lax.psum(1, MP)
    rows, cols = trainer_up.shape
    piece = cols // n_mp
    up_half = trainer_up.astype(jnp.bfloat16).reshape(rows, n_mp, piece).transpose(1, 0, 2)
    up_cols = lax.all_to_all(up_half, MP, 0, 0, tiled=True).reshape(n_mp * rows, piece)
    up_mine = lax.all_gather(up_cols, "rep", axis=1, tiled=True)
    up_other = lax.ppermute(up_mine, "core", [(0, 1), (1, 0)])
    w_up = jnp.concatenate([up_mine, up_other], axis=1)
    frows, dcols = trainer_down.shape
    down_half = trainer_down.astype(jnp.bfloat16).reshape(n_mp, piece, dcols)
    down_rows = lax.all_to_all(down_half, MP, 0, 0, tiled=True)
    down_rows = (
        down_rows.reshape(n_mp, piece, dcols).transpose(1, 0, 2).reshape(piece, n_mp * dcols)
    )
    down_mine = lax.all_gather(down_rows, "rep", axis=0, tiled=True)
    down_other = lax.ppermute(down_mine, "core", [(0, 1), (1, 0)])
    w_down = jnp.concatenate([down_mine, down_other], axis=0)
    x_all = lax.all_gather(xin, "mc", axis=0, tiled=True)
    hidden = jax.nn.gelu(
        jnp.dot(x_all, w_up, preferred_element_type=jnp.float32), approximate=True
    ).astype(jnp.bfloat16)
    mlp = lax.psum_scatter(
        jnp.dot(hidden, w_down, preferred_element_type=jnp.float32).astype(jnp.bfloat16),
        "mc",
        scatter_dimension=0,
        tiled=True,
    ).astype(jnp.float32)
    result = as_float + gate * mlp
    return result.astype(jnp.bfloat16)[None]


def solution(mesh):
    n_rep, n_mp = mesh.devices.shape
    chips = Mesh(mesh.devices.reshape(n_rep, n_mp // 2, 2), ("rep", "mc", "core"))
    in_specs = (
        P("rep", MP, None),
        P("rep", MP),
        P("rep", None, None, None),
        P(MP, "rep"),
        P("rep", MP),
    )
    out_specs = P("rep", MP, None)
    return jax.shard_map(local, mesh=chips, in_specs=in_specs, out_specs=out_specs, check_vma=False)
```

profile of v0, /device:TPU:1, one launch (start us, length us, event | category | flops | bytes accessed | tf_op | source)
XLA Modules:
  0.0 585.3 jit_solution(13966599562315707756)
XLA Ops:
  6.5 1.3 convert_element_type.31
  7.9 0.3 copy.13
  8.2 0.3 reshape.28
  8.5 37.6 %all_to_all.10 = bf16[32,160,54]{1,2,0:T(8,128)(2,1)S(1)} all-to-all(bf16[32,160,54]{1,2,0:T(8,128)(2,1)S(1)} %bitcast.65), channel_id=1, replica_groups=mesh['rep'=8,'mc'=16,'core'=2] {'mc','core'}, dimensions={0} | all-to-all | bytes 1105920 | tf_op jit(solution)/shard_map/all_to_all | solution.py:29
  46.3 2.3 reshape.29
  48.8 0.3 copy.15
  49.1 0.3 reshape.30
  49.4 41.0 %all_to_all.11 = bf16[32,54,160]{2,1,0:T(8,128)(2,1)S(1)} all-to-all(bf16[32,54,160]{2,1,0:T(8,128)(2,1)S(1)} %reshape.30), channel_id=1, replica_groups=mesh['rep'=8,'mc'=16,'core'=2] {'mc','core'}, dimensions={0} | all-to-all | bytes 1105920 | tf_op jit(solution)/shard_map/all_to_all | solution.py:35
  90.6 2.3 reshape.34
  93.2 0.3 fusion.21
  93.5 1.8 fusion.28
  95.3 1.9 copy-done
  97.3 1.2 fusion.27
  98.5 65.6 %all-gather.8.cloned.1.call-done = bf16[8,54,5120]{2,1,0:T(8,128)(2,1)} async-done(((bf16[1,54,5120]{2,1,0:T(8,128)(2,1)}), bf16[8,54,5120]{2,1,0:T(8,128)(2,1)}) %all-gather.8.cloned.1.call-update) | async-done | bytes 4423696 | tf_op jit(solution)/shard_map/all_gather | solution.py:30
  164.2 4.3 reshape.33
  168.5 0.5 collective-permute-start
  169.0 97.5 %all-gather.10.cloned.1.call-done = bf16[8,54,5120]{2,1,0:T(8,128)(2,1)} async-done(((bf16[1,54,5120]{2,1,0:T(8,128)(2,1)}), bf16[8,54,5120]{2,1,0:T(8,128)(2,1)}) %all-gather.10.cloned.1.call-update) | async-done | bytes 4423696 | tf_op jit(solution)/shard_map/all_gather | solution.py:39
  266.5 4.4 reshape.35
  270.9 0.9 collective-permute-start.1
  271.8 131.1 %all-gather.6.cloned.1.call-done = bf16[1024,5120]{1,0:T(8,128)(2,1)} async-done(((bf16[64,5120]{1,0:T(8,128)(2,1)}), bf16[1024,5120]{1,0:T(8,128)(2,1)}) %all-gather.6.cloned.1.call-update) | async-done | bytes 10485776 | tf_op jit(solution)/shard_map/all_gather | solution.py:42
  402.9 15.4 %fusion.14 = bf16[1024,864]{0,1:T(8,128)(2,1)S(1)} fusion(bf16[1024,5120]{1,0:T(8,128)(2,1)} %all-gather.6.cloned.1.call-done, bf16[5120,432]{0,1:T(8,128)(2,1)} %collective-permute-done, bf16[5120,432]{0,1:T(8,128)(2,1)} %bitcast.64), kind=kOutput, calls=%fused_computation.16 | convolution fusion | flops 9085353984 | bytes 21102592 | tf_op jit(solution)/shard_map/dot_general | solution.py:44
  418.4 16.2 %convolution_convert_fusion = bf16[1024,5120]{1,0:T(8,128)(2,1)} fusion(bf16[1024,864]{0,1:T(8,128)(2,1)S(1)} %fusion.14, bf16[432,5120]{1,0:T(8,128)(2,1)} %collective-permute-done.1, bf16[432,5120]{1,0:T(8,128)(2,1)S(1)} %copy-done.2), kind=kOutput, calls=%fused_computation | convolution fusion | flops 9082634240 | bytes 21102592 | tf_op jit(solution)/shard_map/dot_general | solution.py:47
  434.6 141.7 %reduce-scatter.2.cloned.1.call-done = bf16[64,5120]{1,0:T(8,128)(2,1)} async-done(((bf16[1024,5120]{1,0:T(8,128)(2,1)}), bf16[64,5120]{1,0:T(8,128)(2,1)}) %reduce-scatter.2.cloned.1.call-update) | async-done | bytes 655376 | tf_op jit(solution)/shard_map/reduce_scatter | solution.py:46
  576.2 2.6 fusion.31
  (27 shorter events, 0.9 us)
Async XLA Ops:
  6.5 157.6 %all-gather.8.cloned.1.call-start = ((), (), s32[]{:S(2)}) async-start(), calls=%async_computation.5 | async-start | bytes 5160960 | tf_op jit(solution)/shard_map/all_gather | solution.py:30
  8.4 40.3 %copy-start.4 = (f32[1728,160]{0,1:T(8,128)S(1)}, f32[1728,160]{0,1:T(8,128)}, u32[]{:S(2)}) copy-start(f32[1728,160]{0,1:T(8,128)} %param.9) | copy-start | bytes 3317764
  48.7 217.8 %all-gather.10.cloned.1.call-start = ((), (), s32[]{:S(2)}) async-start(), calls=%async_computation.6 | async-start | bytes 5160960 | tf_op jit(solution)/shard_map/all_gather | solution.py:39
  49.1 43.8 %copy-start.1 = (bf16[1,64,5120]{2,1,0:T(8,128)(2,1)S(1)}, bf16[1,64,5120]{2,1,0:T(8,128)(2,1)}, u32[]{:S(2)}) copy-start(bf16[1,64,5120]{2,1,0:T(8,128)(2,1)} %param.5) | copy-start | bytes 1966084
  49.4 44.1 %copy-start.3 = (f32[1,12,3,5120]{3,0,2,1:T(1,128)S(1)}, f32[1,12,3,5120]{3,0,2,1:T(1,128)}, u32[]{:S(2)}) copy-start(f32[1,12,3,5120]{3,0,2,1:T(1,128)} %param.7) | copy-start | bytes 2211844
  49.4 44.1 %copy-start.5 = (s32[1,64]{1,0:T(1,128)S(1)}, s32[1,64]{1,0:T(1,128)}, u32[]{:S(2)}) copy-start(s32[1,64]{1,0:T(1,128)} %param.6) | copy-start | bytes 772
  92.9 310.0 %all-gather.6.cloned.1.call-start = ((), (), s32[]{:S(2)}) async-start(), calls=%async_computation.3 | async-start | bytes 11141120 | tf_op jit(solution)/shard_map/all_gather | solution.py:42
  95.3 1.9 copy-start
  98.5 477.7 %reduce-scatter.2.cloned.1.call-start = ((), (), s32[]{:S(2)}) async-start(), calls=%async_computation.4 | async-start | bytes 11141120 | tf_op jit(solution)/shard_map/reduce_scatter | solution.py:46
  168.5 103.3 %collective-permute-start = (bf16[5120,432]{0,1:T(8,128)(2,1)}, bf16[5120,432]{0,1:T(8,128)(2,1)}, u32[]{:S(2)}, u32[]{:S(2)}) collective-permute-start(bf16[5120,432]{0,1:T(8,128)(2,1)} %bitcast.63), channel_id=1, source_target_pairs={{0,1},{1,0},{2,3},{3,2},{4,5},{5,4},{6,7},{7,6},{8,9},{9,8},{10,11... | collective-permute-start | bytes 13271048 | tf_op jit(solution)/shard_map/ppermute | solution.py:31
  270.9 147.5 %collective-permute-start.1 = (bf16[432,5120]{1,0:T(8,128)(2,1)}, bf16[432,5120]{1,0:T(8,128)(2,1)}, u32[]{:S(2)}, u32[]{:S(2)}) collective-permute-start(bf16[432,5120]{1,0:T(8,128)(2,1)} %reshape.35), channel_id=1, source_target_pairs={{0,1},{1,0},{2,3},{3,2},{4,5},{5,4},{6,7},{7,6},{8,9},{9,8},{10,11... | collective-permute-start | bytes 13271048 | tf_op jit(solution)/shard_map/ppermute | solution.py:40
  402.9 15.5 %copy-start.2 = (bf16[432,5120]{1,0:T(8,128)(2,1)S(1)}, bf16[432,5120]{1,0:T(8,128)(2,1)}, u32[]{:S(2)}) copy-start(bf16[432,5120]{1,0:T(8,128)(2,1)} %reshape.35) | copy-start | bytes 13271044
Sparse Core Ops, SparseCore 0:
  48.8 115.3 all-gather.7
  166.0 100.4 all-gather.9
  268.9 133.9 all-gather.5
  434.7 141.4 reduce-scatter.1
where the time goes:
time: 586 us; the launch traced here: 585 us
  waiting for transfers between devices  436 us (74%)
  blocking collectives  78.6 us (13%)
  matrix products  33.4 us (6%)
  local copies, waits for them, and re-layouts  16.9 us (3%)
  between operations  13.3 us (2%)
    reduce_scatter x1, waiting for transfers between devices, local(): lax.psum_scatter(jnp.dot(hidden, w_down, preferred_element_type=jnp.float...  142 us
    all_gather x1, waiting for transfers between devices, local(): x_all = lax.all_gather(xin, 'mc', axis=0, tiled=True)  131 us
    all_gather x1, waiting for transfers between devices, local(): down_mine = lax.all_gather(down_rows, 'rep', axis=0, tiled=True)  97.5 us
    all_gather x1, waiting for transfers between devices, local(): up_mine = lax.all_gather(up_cols, 'rep', axis=1, tiled=True)  65.6 us
    all_to_all x1, blocking collectives, local(): down_rows = lax.all_to_all(down_half, MP, 0, 0, tiled=True)  41 us
    all_to_all x1, blocking collectives, local(): lax.all_to_all(up_half, MP, 0, 0, tiled=True).reshape(n_mp * rows, piece)  37.6 us
    dot_general x1, matrix products, local(): jnp.dot(hidden, w_down, preferred_element_type=jnp.float32)  16.2 us
    dot_general x1, matrix products, local(): jnp.dot(x_all, w_up, preferred_element_type=jnp.float32)  15.4 us
  transfers between devices with their start and end apart: 6, of which 4 were waited for; matrix products, arithmetic and copies ran while one was open for 5% of the time, Pallas kernels for 0%

commit v1 on v0

--- a/solution.py
+++ b/solution.py
@@ -39,7 +39,9 @@
     down_mine = lax.all_gather(down_rows, "rep", axis=0, tiled=True)
     down_other = lax.ppermute(down_mine, "core", [(0, 1), (1, 0)])
     w_down = jnp.concatenate([down_mine, down_other], axis=0)
-    x_all = lax.all_gather(xin, "mc", axis=0, tiled=True)
+    x_all = jnp.concatenate(
+        lax.all_to_all(jnp.stack([xin] * lax.axis_size("mc")), "mc", 0, 0), axis=0
+    )
     hidden = jax.nn.gelu(
         jnp.dot(x_all, w_up, preferred_element_type=jnp.float32), approximate=True
     ).astype(jnp.bfloat16)

time: 586 us -> 674 us (1.15)
  waiting for transfers between devices: 436 us -> 571 us
  blocking collectives: 78.6 us -> 0 us
  starting transfers between devices: 1.52 us -> 25.2 us
    all_gather x1, waiting for transfers between devices: 65.6 us -> 288 us  [local(): up_mine = lax.all_gather(up_cols, 'rep', axis=1, tiled=True)]
    all_gather x1 -> x0, waiting for transfers between devices: 131 us -> none  [local(): x_all = lax.all_gather(xin, 'mc', axis=0, tiled=True)]
    all_to_all x2 -> x0, blocking collectives: 78.6 us -> none  [the longest x1 41 us: local(): down_rows = lax.all_to_all(down_half, MP, 0, 0, tiled=True)]
    all_to_all x0 -> x3, waiting for transfers between devices: none -> 41.6 us  [the longest x1 23.8 us: local(): down_rows = lax.all_to_all(down_half, MP, 0, 0, tiled=True)]
    all_to_all x0 -> x3, starting transfers between devices: none -> 24.1 us  [the longest x1 12.9 us: local(): lax.all_to_all(up_half, MP, 0, 0, tiled=True).reshape(n_mp * rows, piece)]
  transfers between devices with their start and end apart: 6 -> 8, of which waited for: 4 -> 5; matrix products, arithmetic and copies ran while one was open for 5% -> 6% of each run, Pallas kernels for 0% -> 0%
where the time goes in v1:
time: 674 us
  waiting for transfers between devices  571 us (85%)
  matrix products  35.2 us (5%)
  starting transfers between devices  25.2 us (4%)
  local copies, waits for them, and re-layouts  21.9 us (3%)
  between operations  13.2 us (2%)
  other arithmetic  7.83 us (1%)
    all_gather x1, waiting for transfers between devices, local(): up_mine = lax.all_gather(up_cols, 'rep', axis=1, tiled=True)  288 us
    reduce_scatter x1, waiting for transfers between devices, local(): lax.psum_scatter(jnp.dot(hidden, w_down, preferred_element_type=jnp.float...  138 us
    all_gather x1, waiting for transfers between devices, local(): down_mine = lax.all_gather(down_rows, 'rep', axis=0, tiled=True)  103 us
    all_to_all x1, waiting for transfers between devices, local(): down_rows = lax.all_to_all(down_half, MP, 0, 0, tiled=True)  23.8 us
    all_to_all x1, waiting for transfers between devices, local(): lax.all_to_all(up_half, MP, 0, 0, tiled=True).reshape(n_mp * rows, piece)  17.8 us
    dot_general x1, matrix products, local(): jnp.dot(hidden, w_down, preferred_element_type=jnp.float32)  16.2 us
    dot_general x1, matrix products, local(): jnp.dot(x_all, w_up, preferred_element_type=jnp.float32)  15.4 us
  transfers between devices with their start and end apart: 8, of which 5 were waited for; matrix products, arithmetic and copies ran while one was open for 6% of the time, Pallas kernels for 0%

profile of v1, /device:TPU:1, one launch (start us, length us, event | category | flops | bytes accessed | tf_op | source)
XLA Modules:
  0.0 673.9 jit_solution(15452978305372123046)
XLA Ops:
  6.5 1.3 convert_element_type.33
  8.2 1.2 reshape.58
  9.4 12.9 %all-to-all-start.1 = ((bf16[32,160,54]{1,2,0:T(8,128)(2,1)}), bf16[32,160,54]{1,2,0:T(8,128)(2,1)S(1)}, u32[]{:S(2)}, u32[]{:S(2)}) async-start(bf16[32,160,54]{1,2,0:T(8,128)(2,1)} %bitcast.9), calls=%async_computation.1 | async-start | bytes 1835008 | tf_op jit(solution)/shard_map/all_to_all | solution.py:29
  22.3 1.3 convert_element_type.35
  23.9 1.2 reshape.60
  25.8 3.6 fusion.28
  29.4 17.8 %all-to-all-done.1 = bf16[32,160,54]{1,2,0:T(8,128)(2,1)S(1)} async-done(((bf16[32,160,54]{1,2,0:T(8,128)(2,1)}), bf16[32,160,54]{1,2,0:T(8,128)(2,1)S(1)}, u32[]{:S(2)}, u32[]{:S(2)}) %all-to-all-start.1) | async-done | bytes 552992 | tf_op jit(solution)/shard_map/all_to_all | solution.py:29
  47.2 6.4 all-to-all-start.2
  53.6 2.1 fusion.32
  55.7 23.8 %all-to-all-done.2 = bf16[32,54,160]{2,1,0:T(8,128)(2,1)S(1)} async-done(((bf16[32,54,160]{2,1,0:T(8,128)(2,1)}), bf16[32,54,160]{2,1,0:T(8,128)(2,1)S(1)}, u32[]{:S(2)}, u32[]{:S(2)}) %all-to-all-start.2) | async-done | bytes 552992 | tf_op jit(solution)/shard_map/all_to_all | solution.py:35
  79.5 5.1 stack.5
  84.6 4.8 all-to-all-start
  89.7 2.3 reshape.59
  92.3 2.3 reshape.64
  94.7 288.2 %all-gather.5.cloned.1.call-done = bf16[8,54,5120]{2,1,0:T(8,128)(2,1)} async-done(((bf16[1,54,5120]{2,1,0:T(8,128)(2,1)}), bf16[8,54,5120]{2,1,0:T(8,128)(2,1)}) %all-gather.5.cloned.1.call-update) | async-done | bytes 4423696 | tf_op jit(solution)/shard_map/all_gather | solution.py:30
  382.8 4.3 reshape.63
  387.1 0.5 collective-permute-start
  387.6 102.6 %all-gather.7.cloned.1.call-done = bf16[8,54,5120]{2,1,0:T(8,128)(2,1)} async-done(((bf16[1,54,5120]{2,1,0:T(8,128)(2,1)}), bf16[8,54,5120]{2,1,0:T(8,128)(2,1)}) %all-gather.7.cloned.1.call-update) | async-done | bytes 4423696 | tf_op jit(solution)/shard_map/all_gather | solution.py:39
  490.2 4.4 reshape.65
  494.6 0.4 collective-permute-start.1
  495.1 15.4 %fusion.14 = bf16[1024,864]{0,1:T(8,128)(2,1)S(1)} fusion(bf16[1024,5120]{1,0:T(8,128)(2,1)} %bitcast.8, bf16[5120,432]{0,1:T(8,128)(2,1)} %collective-permute-done, bf16[5120,432]{0,1:T(8,128)(2,1)} %bitcast.63), kind=kOutput, calls=%fused_computation.16 | convolution fusion | flops 9085353984 | bytes 21102592 | tf_op jit(solution)/shard_map/dot_general | solution.py:46
  510.5 16.2 %convolution_convert_fusion = bf16[1024,5120]{1,0:T(8,128)(2,1)} fusion(bf16[1024,864]{0,1:T(8,128)(2,1)S(1)} %fusion.14, bf16[432,5120]{1,0:T(8,128)(2,1)} %collective-permute-done.1, bf16[432,5120]{1,0:T(8,128)(2,1)S(1)} %copy-done.1), kind=kOutput, calls=%fused_computation | convolution fusion | flops 9082634240 | bytes 21102592 | tf_op jit(solution)/shard_map/dot_general | solution.py:49
  526.7 138.1 %reduce-scatter.2.cloned.1.call-done = bf16[64,5120]{1,0:T(8,128)(2,1)} async-done(((bf16[1024,5120]{1,0:T(8,128)(2,1)}), bf16[64,5120]{1,0:T(8,128)(2,1)}) %reduce-scatter.2.cloned.1.call-update) | async-done | bytes 655376 | tf_op jit(solution)/shard_map/reduce_scatter | solution.py:48
  664.9 2.6 fusion.31
  (25 shorter events, 1.8 us)
Async XLA Ops:
  9.4 15.8 %copy-start = (bf16[1,64,5120]{2,1,0:T(8,128)(2,1)S(1)}, bf16[1,64,5120]{2,1,0:T(8,128)(2,1)}, u32[]{:S(2)}) copy-start(bf16[1,64,5120]{2,1,0:T(8,128)(2,1)} %param.5) | copy-start | bytes 1966084
  9.4 37.8 %all-to-all-start.1 = ((bf16[32,160,54]{1,2,0:T(8,128)(2,1)}), bf16[32,160,54]{1,2,0:T(8,128)(2,1)S(1)}, u32[]{:S(2)}, u32[]{:S(2)}) async-start(bf16[32,160,54]{1,2,0:T(8,128)(2,1)} %bitcast.9), calls=%async_computation.1 | async-start | bytes 1835008 | tf_op jit(solution)/shard_map/all_to_all | solution.py:29
  22.3 3.5 copy-start.3
  23.9 1.8 copy-start.2
  47.2 32.3 %all-to-all-start.2 = ((bf16[32,54,160]{2,1,0:T(8,128)(2,1)}), bf16[32,54,160]{2,1,0:T(8,128)(2,1)S(1)}, u32[]{:S(2)}, u32[]{:S(2)}) async-start(bf16[32,54,160]{2,1,0:T(8,128)(2,1)} %reshape.60), calls=%async_computation.2 | async-start | bytes 1835008 | tf_op jit(solution)/shard_map/all_to_all | solution.py:35
  84.6 410.4 %all-to-all-start = ((bf16[16,64,5120]{2,1,0:T(8,128)(2,1)}), bf16[16,64,5120]{2,1,0:T(8,128)(2,1)}, u32[]{:S(2)}, u32[]{:S(2)}) async-start(bf16[16,64,5120]{2,1,0:T(8,128)(2,1)} %stack.5), calls=%async_computation | async-start | bytes 20971520 | tf_op jit(solution)/shard_map/all_to_all | solution.py:43
  89.4 293.4 %all-gather.5.cloned.1.call-start = ((), (), s32[]{:S(2)}) async-start(), calls=%async_computation.5 | async-start | bytes 5160960 | tf_op jit(solution)/shard_map/all_gather | solution.py:30
  92.0 398.2 %all-gather.7.cloned.1.call-start = ((), (), s32[]{:S(2)}) async-start(), calls=%async_computation.6 | async-start | bytes 5160960 | tf_op jit(solution)/shard_map/all_gather | solution.py:39
  94.6 570.2 %reduce-scatter.2.cloned.1.call-start = ((), (), s32[]{:S(2)}) async-start(), calls=%async_computation.4 | async-start | bytes 11141120 | tf_op jit(solution)/shard_map/reduce_scatter | solution.py:48
  387.1 107.9 %collective-permute-start = (bf16[5120,432]{0,1:T(8,128)(2,1)}, bf16[5120,432]{0,1:T(8,128)(2,1)}, u32[]{:S(2)}, u32[]{:S(2)}) collective-permute-start(bf16[5120,432]{0,1:T(8,128)(2,1)} %bitcast.62), channel_id=1, source_target_pairs={{0,1},{1,0},{2,3},{3,2},{4,5},{5,4},{6,7},{7,6},{8,9},{9,8},{10,11... | collective-permute-start | bytes 13271048 | tf_op jit(solution)/shard_map/ppermute | solution.py:31
  494.6 15.9 %collective-permute-start.1 = (bf16[432,5120]{1,0:T(8,128)(2,1)}, bf16[432,5120]{1,0:T(8,128)(2,1)}, u32[]{:S(2)}, u32[]{:S(2)}) collective-permute-start(bf16[432,5120]{1,0:T(8,128)(2,1)} %reshape.65), channel_id=1, source_target_pairs={{0,1},{1,0},{2,3},{3,2},{4,5},{5,4},{6,7},{7,6},{8,9},{9,8},{10,11... | collective-permute-start | bytes 13271048 | tf_op jit(solution)/shard_map/ppermute | solution.py:40
  495.0 15.5 %copy-start.1 = (bf16[432,5120]{1,0:T(8,128)(2,1)S(1)}, bf16[432,5120]{1,0:T(8,128)(2,1)}, u32[]{:S(2)}) copy-start(bf16[432,5120]{1,0:T(8,128)(2,1)} %reshape.65) | copy-start | bytes 13271044
Sparse Core Ops, SparseCore 0:
  92.1 290.6 all-gather.4
  384.6 105.5 all-gather.6
  526.8 137.9 reduce-scatter.1
